TPU v7x, 128 devices: a whole 4x4x4 slice. The times are simulated.
128 devices in a mesh: dp: 8 (over y, core), ctx: 16 (over z, x).
Axes of the slice: x: 4, y: 4, z: 4, core: 2. Of those that a mesh axis runs over, the one named last changes fastest.
Arguments:
- queries: bfloat16 [8, 4096, 256], P('dp', 'ctx'), may hold values from -6 to 6
- keys: bfloat16 [8, 4096, 256], P('dp', 'ctx'), may hold values from -6 to 6
- values: bfloat16 [8, 4096, 256], P('dp', 'ctx'), may hold values from -6 to 6
- grad_out: bfloat16 [8, 4096, 256], P('dp', 'ctx'), may hold values from -6 to 6
- log_norm: float32 [8, 2, 4096], P('dp', None, 'ctx'), may hold values from 5 to 7
- offsets: int32 [2, 5], replicated, may hold values from 0 to 15
- q_gain: float32 [256], replicated, may hold values from 0.5 to 2
Outputs:
- grad_queries: bfloat16 [8, 4096, 256], P('dp', 'ctx')
- grad_keys: bfloat16 [8, 4096, 256], P('dp', 'ctx')
- grad_values: bfloat16 [8, 4096, 256], P('dp', 'ctx')
- grad_gain: float32 [256], replicated
All inputs are finite; a program needn't handle non-finite values.
Results may differ from a plain program's by a relative error of at most 0.013.
The roundings to bfloat16 on the way count: a program that leaves them out, or rounds other values in their place, can miss the bound.
Values may be sent and summed in bfloat16 or wider, within the bound.
No kernel may reach another device: no remote copies, remote signals or barrier semaphores. Data moves between devices by JAX's collectives and lax.ppermute only.
A program may use at most 64 MiB of HBM per device.

v0:
```python
import math
import jax
import jax.numpy as jnp
from jax import lax
from jax.sharding import PartitionSpec as P

BLOCK = 128
LEVELS = 5


def swapped(block, axis, stride):
    count = lax.axis_size(axis)
    route = []
    for low in range(count):
        high = low | 1 << stride
        if high != low and high < count:
            route += [(low, high), (high, low)]
    return lax.ppermute(block, axis, route)


def slot_table(device_local, offset_vec, stride, block_count):
    slot_count = (block_count + stride - 1) // stride
    base_block = device_local * block_count + jnp.zeros_like(offset_vec)
    first_step = jnp.maximum((base_block - offset_vec + stride - 1) // stride, 0)
    step_index = first_step[..., None] + jnp.arange(slot_count, dtype=jnp.int32)
    global_block = offset_vec[..., None] + stride * step_index
    local_block = global_block - base_block[..., None]
    usable = (step_index < block_count) & (local_block >= 0) & (local_block < block_count)
    return (jnp.clip(local_block, 0, block_count - 1), usable.astype(jnp.float32))


def segment_slots(shift_vec, span_len, block_count):
    device_col = jnp.arange(span_len, dtype=jnp.int32)[:, None]
    seg_block, seg_usable = slot_table(device_col, shift_vec[None, :], span_len, block_count)
    return (seg_block.transpose(1, 0, 2), seg_usable.transpose(1, 0, 2))


def select_table(local_block, block_count):
    return (local_block[..., None] == jnp.arange(block_count, dtype=jnp.int32)).astype(jnp.float32)


def pick_blocks(data, table):
    head_count, block_count = (data.shape[0], data.shape[1])
    flat = data.reshape(head_count, block_count, -1).astype(jnp.float32)
    chosen = jnp.einsum(
        "hsb,hbx->hsx",
        table,
        flat,
        precision=lax.Precision.HIGHEST,
        preferred_element_type=jnp.float32,
    ).astype(data.dtype)
    return chosen.reshape((head_count, -1) + data.shape[3:])


def place_rows(accum, contrib, table, usable):
    head_count, block_count = (accum.shape[0], accum.shape[1])
    slot_count = table.shape[1]
    weights = table * usable[..., None]
    shaped = contrib.reshape(head_count, slot_count, -1)
    added = jnp.einsum(
        "hsb,hsx->hbx",
        weights,
        shaped,
        precision=lax.Precision.HIGHEST,
        preferred_element_type=jnp.float32,
    )
    return accum + added.reshape(accum.shape)


def attend(
    query_rows,
    dout_rows,
    norm_rows,
    query_mask,
    key_rows,
    value_rows,
    key_mask,
    score_scale,
    row_block,
):
    head_count, query_count, head_dim = query_rows.shape
    steps = query_count // row_block

    def split(array):
        return jnp.moveaxis(array.reshape((head_count, steps, row_block) + array.shape[2:]), 1, 0)

    def step_fn(carry, parts):
        query_blk, dout_blk, norm_blk, mask_blk = parts
        scores = (
            jnp.einsum("hqd,hkd->hqk", query_blk, key_rows, preferred_element_type=jnp.float32)
            * score_scale
        )
        probs = jnp.exp(scores - norm_blk[:, :, None]) * mask_blk[:, :, None] * key_mask[:, None, :]
        probs_low = probs.astype(jnp.bfloat16)
        prob_grad = jnp.einsum(
            "hqd,hkd->hqk", dout_blk, value_rows, preferred_element_type=jnp.float32
        )
        dscore = (probs * prob_grad).astype(jnp.bfloat16)
        query_grad = (
            jnp.einsum("hqk,hkd->hqd", dscore, key_rows, preferred_element_type=jnp.float32)
            * score_scale
        )
        key_part = (
            jnp.einsum("hqk,hqd->hkd", dscore, query_blk, preferred_element_type=jnp.float32)
            * score_scale
        )
        value_part = jnp.einsum(
            "hqk,hqd->hkd", probs_low, dout_blk, preferred_element_type=jnp.float32
        )
        return ((carry[0] + key_part, carry[1] + value_part), query_grad)

    start = jnp.zeros((head_count, key_rows.shape[1], head_dim), jnp.float32)
    totals, query_parts = lax.scan(
        step_fn,
        (start, start),
        (split(query_rows), split(dout_rows), split(norm_rows), split(query_mask)),
    )
    query_grad = jnp.moveaxis(query_parts, 0, 1).reshape(head_count, query_count, head_dim)
    return (query_grad, totals[0], totals[1])


def swap_up(payload, my_index, bit_total):
    for bit_idx in range(bit_total):
        partner = swapped(payload, "ctx", bit_idx)
        lower_half = my_index >> bit_idx & 1 == 0
        payload = jnp.where(
            lower_half,
            jnp.concatenate([payload, partner], axis=1),
            jnp.concatenate([partner, payload], axis=1),
        )
    return payload


def swap_down(sums_kv, my_index, bit_total):
    head_count = sums_kv.shape[0]
    for bit_idx in reversed(range(bit_total)):
        halves = sums_kv.reshape(head_count, 2, -1, sums_kv.shape[-1])
        lower_half = my_index >> bit_idx & 1 == 0
        kept_half = jnp.where(lower_half, halves[:, 0], halves[:, 1])
        sent_half = jnp.where(lower_half, halves[:, 1], halves[:, 0])
        sums_kv = kept_half + swapped(sent_half.astype(jnp.bfloat16), "ctx", bit_idx).astype(
            sent_half.dtype
        )
    return sums_kv


def body(queries, keys, values, grad_out, log_norm, offsets, q_gain):
    query_raw = queries[0]
    token_count, proj_width = query_raw.shape
    head_count = log_norm.shape[1]
    head_dim = proj_width // head_count
    block_count = token_count // BLOCK
    ctx_size = lax.axis_size("ctx")
    score_scale = head_dim ** (-0.5)
    scaled = (query_raw.astype(jnp.float32) * q_gain).astype(jnp.bfloat16)

    def heads(matrix):
        return (
            matrix.reshape(token_count, head_count, head_dim)
            .transpose(1, 0, 2)
            .reshape(head_count, block_count, BLOCK, head_dim)
        )

    query_all = heads(scaled)
    key_all = heads(keys[0])
    value_all = heads(values[0])
    dout_all = heads(grad_out[0])
    norm_all = log_norm[0].reshape(head_count, block_count, BLOCK)
    query_acc = jnp.zeros((head_count, block_count, BLOCK, head_dim), jnp.float32)
    kv_acc = jnp.zeros((head_count, block_count, BLOCK, 2 * head_dim), jnp.float32)
    my_index = lax.axis_index("ctx")
    for level_idx in range(LEVELS):
        span_len = min(2**level_idx, ctx_size)
        shift_vec = offsets[:, level_idx] % span_len
        local_block, usable = slot_table(my_index % span_len, shift_vec, span_len, block_count)
        table = select_table(local_block, block_count)
        slot_count = local_block.shape[1]
        row_block = BLOCK * math.gcd(slot_count, max(1, 512 // BLOCK))
        query_own = pick_blocks(query_all, table)
        dout_own = pick_blocks(dout_all, table)
        norm_own = pick_blocks(norm_all, table)
        mask_own = jnp.repeat(usable, BLOCK, axis=1)
        payload = jnp.concatenate(
            [pick_blocks(key_all, table), pick_blocks(value_all, table)], axis=2
        )
        bit_total = span_len.bit_length() - 1
        payload = swap_up(payload, my_index, bit_total)
        seg_block, seg_usable = segment_slots(shift_vec, span_len, block_count)
        seg_mask = jnp.repeat(seg_usable.reshape(head_count, -1), BLOCK, axis=1)
        level_query, level_key, level_value = attend(
            query_own,
            dout_own,
            norm_own,
            mask_own,
            payload[..., :head_dim],
            payload[..., head_dim:],
            seg_mask,
            score_scale,
            row_block,
        )
        sums_kv = jnp.concatenate([level_key, level_value], axis=2)
        sums_kv = swap_down(sums_kv, my_index, bit_total)
        query_acc = place_rows(query_acc, level_query, table, usable)
        kv_acc = place_rows(kv_acc, sums_kv, table, usable)

    def to_rows(field_acc):
        return (
            field_acc.reshape(head_count, token_count, -1)
            .transpose(1, 0, 2)
            .reshape(token_count, -1)
        )

    dq_rows = to_rows(query_acc)
    grad_queries = (dq_rows * q_gain).astype(jnp.bfloat16)
    grad_keys = to_rows(kv_acc[..., :head_dim]).astype(jnp.bfloat16)
    grad_values = to_rows(kv_acc[..., head_dim:]).astype(jnp.bfloat16)
    gain_total = lax.psum(jnp.sum(query_raw.astype(jnp.float32) * dq_rows, axis=0), ("dp", "ctx"))
    return (grad_queries[None], grad_keys[None], grad_values[None], gain_total)


def solution(mesh):
    in_specs = (
        P("dp", "ctx", None),
        P("dp", "ctx", None),
        P("dp", "ctx", None),
        P("dp", "ctx", None),
        P("dp", None, "ctx"),
        P(),
        P(),
    )
    out_specs = (P("dp", "ctx", None), P("dp", "ctx", None), P("dp", "ctx", None), P())
    return jax.shard_map(body, mesh=mesh, in_specs=in_specs, out_specs=out_specs, check_vma=False)
```

profile of v0, /device:TPU:0, one launch (start us, length us, event | category | flops | bytes accessed | tf_op | source)
XLA Modules:
  0.0 272.5 jit_solution(3529592541120777040)
XLA Ops:
  0.7 0.9 reshape_squeeze.12
  1.7 1.7 clamp_reduce_fusion.3
  3.9 0.9 reshape_squeeze.15
  5.4 1.6 collective-permute-start
  9.4 1.6 collective-permute-start.3
  11.9 1.1 collective-permute-start.6
  19.4 0.9 fusion.193
  20.3 0.9 fusion.203
  26.8 1.0 copy.380
  28.0 0.9 reshape_reshape_transpose.2
  28.9 1.2 reshape.1667
  33.0 0.8 copy-done.5
  34.6 3.2 %collective-permute-start.2 = (bf16[2,256,256]{2,1,0:T(8,128)(2,1)S(1)}, bf16[2,256,256]{2,1,0:T(8,128)(2,1)S(1)}, u32[]{:S(2)}, u32[]{:S(2)}) collective-permute-start(bf16[2,256,256]{2,1,0:T(8,128)(2,1)S(1)} %maximum_select_fusion.7), channel_id=1, source_target_pairs={{0,2},{2,0},{1,3},{3,1},{4,6},{6,4},{5,7},{7,5},{8,10},{10,8},{9,1... | collective-permute-start | bytes 786440 | tf_op jit(solution)/shard_map/ppermute | solution.py:18
  37.9 0.8 copy.373
  39.3 0.8 maximum_select_fusion.9
  40.1 2.0 collective-permute-start.7
  42.1 0.8 maximum_select_fusion.8
  42.9 1.5 collective-permute-start.4
  44.5 1.0 collective-permute-done.2
  47.9 9.2 %collective-permute-done.4 = bf16[2,256,256]{2,1,0:T(8,128)(2,1)} collective-permute-done((bf16[2,256,256]{2,1,0:T(8,128)(2,1)}, bf16[2,256,256]{2,1,0:T(8,128)(2,1)}, u32[]{:S(2)}, u32[]{:S(2)}) %collective-permute-start.4) | collective-permute-done | bytes 262176 | tf_op jit(solution)/shard_map/ppermute | solution.py:18
  57.1 1.3 maximum_select_fusion.4
  58.4 2.4 collective-permute-start.5
  60.8 0.8 fusion.213
  62.4 0.8 fusion.49
  63.1 3.0 %collective-permute-start.11 = (bf16[2,256,256]{2,1,0:T(8,128)(2,1)}, bf16[2,256,256]{2,1,0:T(8,128)(2,1)}, u32[]{:S(2)}, u32[]{:S(2)}) collective-permute-start(bf16[2,256,256]{2,1,0:T(8,128)(2,1)} %fusion.49), channel_id=1, source_target_pairs={{0,2},{2,0},{1,3},{3,1},{4,6},{6,4},{5,7},{7,5},{8,10},{10,8},{9,1... | collective-permute-start | bytes 786440 | tf_op jit(solution)/shard_map/ppermute | solution.py:18
  66.1 2.2 maximum_select_fusion.5
  68.4 4.8 %collective-permute-done.5 = bf16[2,512,256]{2,1,0:T(8,128)(2,1)} collective-permute-done((bf16[2,512,256]{2,1,0:T(8,128)(2,1)S(1)}, bf16[2,512,256]{2,1,0:T(8,128)(2,1)}, u32[]{:S(2)}, u32[]{:S(2)}) %collective-permute-start.5) | collective-permute-done | bytes 524320 | tf_op jit(solution)/shard_map/ppermute | solution.py:18
  73.2 1.4 maximum_select_fusion.1
  77.0 1.5 pad_maximum_fusion.1
  78.5 3.0 %reshape.1673 = f32[2,2,512,256]{2,1,3,0:T(2,128)S(1)} reshape(f32[2,1024,256]{1,2,0:T(8,128)} %pad_maximum_fusion.1) | data formatting | bytes 4194304 | tf_op jit(solution)/shard_map/reshape | solution.py:137
  81.6 2.9 %fusion.212 = (f32[2,1,512,256]{2,1,3,0:T(1,128)}, f32[2,1,512,256]{2,1,3,0:T(1,128)}) fusion(f32[2,2,512,256]{2,1,3,0:T(2,128)S(1)} %reshape.1673), kind=kLoop, calls=%fused_computation.413 | loop fusion | bytes 4194304 | tf_op jit(solution)/shard_map/slice | solution.py:139
  84.5 2.3 copy.151
  86.9 2.4 copy.152
  89.4 2.7 collective-permute-start.13
  92.1 1.8 maximum_select_fusion.2
  93.8 3.7 %collective-permute-start.9 = (bf16[2,1024,256]{2,1,0:T(8,128)(2,1)S(1)}, bf16[2,1024,256]{2,1,0:T(8,128)(2,1)S(1)}, u32[]{:S(2)}, u32[]{:S(2)}) collective-permute-start(bf16[2,1024,256]{2,1,0:T(8,128)(2,1)S(1)} %maximum_select_fusion.2), channel_id=1, source_target_pairs={{0,8},{8,0},{1,9},{9,1},{2,10},{10,2},{3,11},{11,3},{4,12},{12,4},... | collective-permute-start | bytes 3145736 | tf_op jit(solution)/shard_map/ppermute | solution.py:18
  97.5 1.0 fusion.58
  98.5 0.9 copy.191
  99.4 1.0 bitcast_add_fusion.5
  100.4 0.7 fusion.68
  101.1 1.7 collective-permute-start.12
  102.8 2.1 collective-permute-done.13
  105.2 18.4 %collective-permute-done.9 = bf16[2,1024,256]{2,1,0:T(8,128)(2,1)S(1)} collective-permute-done((bf16[2,1024,256]{2,1,0:T(8,128)(2,1)S(1)}, bf16[2,1024,256]{2,1,0:T(8,128)(2,1)S(1)}, u32[]{:S(2)}, u32[]{:S(2)}) %collective-permute-start.9) | collective-permute-done | bytes 1048608 | tf_op jit(solution)/shard_map/ppermute | solution.py:18
  127.4 2.5 pad_maximum_fusion
  129.9 6.6 %reshape.1677 = f32[2,2,1024,256]{2,1,3,0:T(2,128)} reshape(f32[2,2048,256]{1,2,0:T(8,128)} %pad_maximum_fusion) | data formatting | bytes 8388608 | tf_op jit(solution)/shard_map/reshape | solution.py:137
  136.5 9.1 %fusion.211 = (f32[2,1,1024,256]{2,1,3,0:T(1,128)}, f32[2,1,1024,256]{2,1,3,0:T(1,128)}) fusion(f32[2,2,1024,256]{2,1,3,0:T(2,128)} %reshape.1677), kind=kLoop, calls=%fused_computation.412 | loop fusion | bytes 8388608 | tf_op jit(solution)/shard_map/slice | solution.py:139
  145.6 4.6 %copy.157 = f32[2,1,1024,256]{3,2,0,1:T(8,128)S(1)} copy(f32[2,1,1024,256]{2,1,3,0:T(1,128)} %get-tuple-element.141) | data formatting | bytes 4194304
  150.2 6.0 %copy.158 = f32[2,1,1024,256]{3,2,0,1:T(8,128)} copy(f32[2,1,1024,256]{2,1,3,0:T(1,128)} %get-tuple-element.142) | data formatting | bytes 4194304
  156.2 1.9 fusion.36
  158.3 3.1 %collective-permute-start.14 = (bf16[2,256,256]{2,1,0:T(8,128)(2,1)S(1)}, bf16[2,256,256]{2,1,0:T(8,128)(2,1)S(1)}, u32[]{:S(2)}, u32[]{:S(2)}) collective-permute-start(bf16[2,256,256]{2,1,0:T(8,128)(2,1)S(1)} %fusion.50), channel_id=1, source_target_pairs={{0,2},{2,0},{1,3},{3,1},{4,6},{6,4},{5,7},{7,5},{8,10},{10,8},{9,1... | collective-permute-start | bytes 786440 | tf_op jit(solution)/shard_map/ppermute | solution.py:18
  161.7 1.1 fusion.55
  162.8 0.9 copy.192
  163.7 3.3 %collective-permute-done.14 = bf16[2,256,256]{2,1,0:T(8,128)(2,1)S(1)} collective-permute-done((bf16[2,256,256]{2,1,0:T(8,128)(2,1)S(1)}, bf16[2,256,256]{2,1,0:T(8,128)(2,1)S(1)}, u32[]{:S(2)}, u32[]{:S(2)}) %collective-permute-start.14) | collective-permute-done | bytes 262176 | tf_op jit(solution)/shard_map/ppermute | solution.py:18
  167.1 0.8 collective-permute-start.15
  167.9 14.9 %collective-permute-done.16 = bf16[2,1024,256]{2,1,0:T(8,128)(2,1)S(1)} collective-permute-done((bf16[2,1024,256]{2,1,0:T(8,128)(2,1)S(1)}, bf16[2,1024,256]{2,1,0:T(8,128)(2,1)S(1)}, u32[]{:S(2)}, u32[]{:S(2)}) %collective-permute-start.16) | collective-permute-done | bytes 1048608 | tf_op jit(solution)/shard_map/ppermute | solution.py:18
  185.6 6.9 %collective-permute-done.17 = bf16[2,512,256]{2,1,0:T(8,128)(2,1)S(1)} collective-permute-done((bf16[2,512,256]{2,1,0:T(8,128)(2,1)S(1)}, bf16[2,512,256]{2,1,0:T(8,128)(2,1)S(1)}, u32[]{:S(2)}, u32[]{:S(2)}) %collective-permute-start.17) | collective-permute-done | bytes 524320 | tf_op jit(solution)/shard_map/ppermute | solution.py:18
  193.5 3.5 %collective-permute-start.18 = (bf16[2,256,256]{2,1,0:T(8,128)(2,1)}, bf16[2,256,256]{2,1,0:T(8,128)(2,1)S(1)}, u32[]{:S(2)}, u32[]{:S(2)}) collective-permute-start(bf16[2,256,256]{2,1,0:T(8,128)(2,1)} %fusion.51), channel_id=1, source_target_pairs={{0,2},{2,0},{1,3},{3,1},{4,6},{6,4},{5,7},{7,5},{8,10},{10,8},{9,1... | collective-permute-start | bytes 786440 | tf_op jit(solution)/shard_map/ppermute | solution.py:18
  197.1 1.2 fusion.6
  199.1 63.0 %psum.7 = f32[256]{0:T(256)} all-reduce(f32[256]{0:T(256)S(1)} %bitcast.569), channel_id=1, replica_groups=mesh['dp'=8,'ctx'=16] {'dp','ctx'}, use_global_device_ids=true, to_apply=%region_1.2 | all-reduce | flops 256 | bytes 2048 | tf_op jit(solution)/shard_map/psum | solution.py:217
  262.3 1.5 collective-permute-start.19
  264.4 3.2 %collective-permute-done.19 = bf16[2,128,256]{2,1,0:T(8,128)(2,1)S(1)} collective-permute-done((bf16[2,128,256]{2,1,0:T(8,128)(2,1)S(1)}, bf16[2,128,256]{2,1,0:T(8,128)(2,1)S(1)}, u32[]{:S(2)}, u32[]{:S(2)}) %collective-permute-start.19) | collective-permute-done | bytes 131104 | tf_op jit(solution)/shard_map/ppermute | solution.py:18
  267.9 2.4 fusion.3
  270.7 0.7 convert_element_type.423
  271.5 0.7 convert_element_type.420
  (296 shorter events, 36.4 us)
Async XLA Ops:
  3.4 5.4 %copy-start.28 = (s32[2]{0:T(128)}, s32[2]{0:T(128)S(1)}, u32[]{:S(2)}) copy-start(s32[2]{0:T(128)S(1)} %get-tuple-element.178) | copy-start | bytes 28
  3.4 5.4 %copy-start.30 = (s32[2]{0:T(128)}, s32[2]{0:T(128)S(1)}, u32[]{:S(2)}) copy-start(s32[2]{0:T(128)S(1)} %get-tuple-element.181) | copy-start | bytes 28
  3.4 5.4 %copy-start.32 = (s32[2]{0:T(128)}, s32[2]{0:T(128)S(1)}, u32[]{:S(2)}) copy-start(s32[2]{0:T(128)S(1)} %get-tuple-element.118) | copy-start | bytes 28
  3.4 5.4 %copy-start.34 = (s32[2]{0:T(128)}, s32[2]{0:T(128)S(1)}, u32[]{:S(2)}) copy-start(s32[2]{0:T(128)S(1)} %get-tuple-element.164) | copy-start | bytes 28
  5.4 26.5 %collective-permute-start = (bf16[2,128,256]{2,1,0:T(8,128)(2,1)S(1)}, bf16[2,128,256]{2,1,0:T(8,128)(2,1)S(1)}, u32[]{:S(2)}, u32[]{:S(2)}) collective-permute-start(bf16[2,128,256]{2,1,0:T(8,128)(2,1)S(1)} %bitcast_dynamic-update-slice_fusion.6), channel_id=1, source_target_pairs={{0,1},{1,0},{2,3},{3,2},{4,5},{5,4},{6,7},{7,6},{8,9},{9,8},{10,11... | collective-permute-start | bytes 393224 | tf_op jit(solution)/shard_map/ppermute | solution.py:18
  7.6 5.4 %copy-start.46 = (f32[1,2,256]{2,1,0:T(2,128)S(1)}, f32[1,2,256]{2,1,0:T(2,128)}, u32[]{:S(2)}) copy-start(f32[1,2,256]{2,1,0:T(2,128)} %param.11) | copy-start | bytes 6148
  7.9 26.5 %collective-permute-start.1 = (bf16[2,128,256]{2,1,0:T(8,128)(2,1)S(1)}, bf16[2,128,256]{2,1,0:T(8,128)(2,1)S(1)}, u32[]{:S(2)}, u32[]{:S(2)}) collective-permute-start(bf16[2,128,256]{2,1,0:T(8,128)(2,1)S(1)} %bitcast_dynamic-update-slice_fusion.4), channel_id=1, source_target_pairs={{0,1},{1,0},{2,3},{3,2},{4,5},{5,4},{6,7},{7,6},{8,9},{9,8},{10,11... | collective-permute-start | bytes 393224 | tf_op jit(solution)/shard_map/ppermute | solution.py:18
  8.5 8.3 %copy-start.25 = (bf16[1,256,256]{2,1,0:T(8,128)(2,1)S(1)}, bf16[1,256,256]{2,1,0:T(8,128)(2,1)}, u32[]{:S(2)}) copy-start(bf16[1,256,256]{2,1,0:T(8,128)(2,1)} %param.10) | copy-start | bytes 393220
  9.4 32.7 %collective-permute-start.3 = (bf16[2,128,256]{2,1,0:T(8,128)(2,1)S(1)}, bf16[2,128,256]{2,1,0:T(8,128)(2,1)S(1)}, u32[]{:S(2)}, u32[]{:S(2)}) collective-permute-start(bf16[2,128,256]{2,1,0:T(8,128)(2,1)S(1)} %bitcast_dynamic-update-slice_fusion.2), channel_id=1, source_target_pairs={{0,1},{1,0},{2,3},{3,2},{4,5},{5,4},{6,7},{7,6},{8,9},{9,8},{10,11... | collective-permute-start | bytes 393224 | tf_op jit(solution)/shard_map/ppermute | solution.py:18
  11.9 27.4 %collective-permute-start.6 = (bf16[2,128,256]{2,1,0:T(8,128)(2,1)S(1)}, bf16[2,128,256]{2,1,0:T(8,128)(2,1)S(1)}, u32[]{:S(2)}, u32[]{:S(2)}) collective-permute-start(bf16[2,128,256]{2,1,0:T(8,128)(2,1)S(1)} %bitcast_dynamic-update-slice_fusion), channel_id=1, source_target_pairs={{0,1},{1,0},{2,3},{3,2},{4,5},{5,4},{6,7},{7,6},{8,9},{9,8},{10,11... | collective-permute-start | bytes 393224 | tf_op jit(solution)/shard_map/ppermute | solution.py:18
  13.0 8.2 %copy-start.57 = (s32[2,2]{1,0:T(2,128)}, s32[2,2]{1,0:T(2,128)S(1)}, u32[]{:S(2)}) copy-start(s32[2,2]{1,0:T(2,128)S(1)} %iota_clamp_fusion) | copy-start | bytes 52
  13.0 8.6 %copy-start.51 = (f32[2,2]{1,0:T(2,128)}, f32[2,2]{1,0:T(2,128)S(1)}, u32[]{:S(2)}) copy-start(f32[2,2]{1,0:T(2,128)S(1)} %and_convert_fusion.8) | copy-start | bytes 52
  24.8 5.3 %copy-start.42 = (s32[2,1]{1,0:T(2,128)S(1)}, s32[2,1]{1,0:T(2,128)}, u32[]{:S(2)}) copy-start(s32[2,1]{1,0:T(2,128)} %get-tuple-element.179) | copy-start | bytes 28
  24.8 5.3 %copy-start.43 = (s32[2,1]{1,0:T(2,128)S(1)}, s32[2,1]{1,0:T(2,128)}, u32[]{:S(2)}) copy-start(s32[2,1]{1,0:T(2,128)} %get-tuple-element.180) | copy-start | bytes 28
  24.9 5.5 %copy-start.40 = (s32[2,1]{1,0:T(2,128)S(1)}, s32[2,1]{1,0:T(2,128)}, u32[]{:S(2)}) copy-start(s32[2,1]{1,0:T(2,128)} %get-tuple-element.176) | copy-start | bytes 28
  24.9 5.5 %copy-start.41 = (s32[2,1]{1,0:T(2,128)S(1)}, s32[2,1]{1,0:T(2,128)}, u32[]{:S(2)}) copy-start(s32[2,1]{1,0:T(2,128)} %get-tuple-element.177) | copy-start | bytes 28
  24.9 5.6 %copy-start.38 = (s32[2,1]{1,0:T(2,128)S(1)}, s32[2,1]{1,0:T(2,128)}, u32[]{:S(2)}) copy-start(s32[2,1]{1,0:T(2,128)} %get-tuple-element.119) | copy-start | bytes 28
  24.9 5.6 %copy-start.39 = (s32[2,1]{1,0:T(2,128)S(1)}, s32[2,1]{1,0:T(2,128)}, u32[]{:S(2)}) copy-start(s32[2,1]{1,0:T(2,128)} %get-tuple-element.120) | copy-start | bytes 28
  24.9 5.7 %copy-start.33 = (s32[2]{0:T(128)S(1)}, s32[2]{0:T(128)}, u32[]{:S(2)}) copy-start(s32[2]{0:T(128)} %copy-done.32) | copy-start | bytes 28
  24.9 5.7 %copy-start.35 = (s32[2]{0:T(128)S(1)}, s32[2]{0:T(128)}, u32[]{:S(2)}) copy-start(s32[2]{0:T(128)} %copy-done.34) | copy-start | bytes 28
  24.9 6.3 %copy-start.29 = (s32[2]{0:T(128)S(1)}, s32[2]{0:T(128)}, u32[]{:S(2)}) copy-start(s32[2]{0:T(128)} %copy-done.28) | copy-start | bytes 28
  24.9 6.3 %copy-start.31 = (s32[2]{0:T(128)S(1)}, s32[2]{0:T(128)}, u32[]{:S(2)}) copy-start(s32[2]{0:T(128)} %copy-done.30) | copy-start | bytes 28
  25.3 6.7 %copy-start.62 = (f32[2,1,128]{2,1,0:T(1,128)S(1)}, f32[2,1,128]{2,1,0:T(1,128)}, u32[]{:S(2)}) copy-start(f32[2,1,128]{2,1,0:T(1,128)} %fusion.197) | copy-start | bytes 3076
  33.0 12.7 %copy-start.61 = (f32[2,1,128]{2,1,0:T(1,128)S(1)}, f32[2,1,128]{2,1,0:T(1,128)}, u32[]{:S(2)}) copy-start(f32[2,1,128]{2,1,0:T(1,128)} %fusion.187) | copy-start | bytes 3076
  34.6 10.8 %collective-permute-start.2 = (bf16[2,256,256]{2,1,0:T(8,128)(2,1)S(1)}, bf16[2,256,256]{2,1,0:T(8,128)(2,1)S(1)}, u32[]{:S(2)}, u32[]{:S(2)}) collective-permute-start(bf16[2,256,256]{2,1,0:T(8,128)(2,1)S(1)} %maximum_select_fusion.7), channel_id=1, source_target_pairs={{0,2},{2,0},{1,3},{3,1},{4,6},{6,4},{5,7},{7,5},{8,10},{10,8},{9,1... | collective-permute-start | bytes 786440 | tf_op jit(solution)/shard_map/ppermute | solution.py:18
  38.7 58.8 %collective-permute-start.10 = (bf16[2,128,256]{2,1,0:T(8,128)(2,1)}, bf16[2,128,256]{2,1,0:T(8,128)(2,1)}, u32[]{:S(2)}, u32[]{:S(2)}) collective-permute-start(bf16[2,128,256]{2,1,0:T(8,128)(2,1)} %fusion.67), channel_id=1, source_target_pairs={{0,1},{1,0},{2,3},{3,2},{4,5},{5,4},{6,7},{7,6},{8,9},{9,8},{10,11... | collective-permute-start | bytes 393224 | tf_op jit(solution)/shard_map/ppermute | solution.py:18
  40.1 26.1 %collective-permute-start.7 = (bf16[2,256,256]{2,1,0:T(8,128)(2,1)}, bf16[2,256,256]{2,1,0:T(8,128)(2,1)}, u32[]{:S(2)}, u32[]{:S(2)}) collective-permute-start(bf16[2,256,256]{2,1,0:T(8,128)(2,1)} %maximum_select_fusion.9), channel_id=1, source_target_pairs={{0,2},{2,0},{1,3},{3,1},{4,6},{6,4},{5,7},{7,5},{8,10},{10,8},{9,1... | collective-permute-start | bytes 786440 | tf_op jit(solution)/shard_map/ppermute | solution.py:18
  42.9 14.2 %collective-permute-start.4 = (bf16[2,256,256]{2,1,0:T(8,128)(2,1)}, bf16[2,256,256]{2,1,0:T(8,128)(2,1)}, u32[]{:S(2)}, u32[]{:S(2)}) collective-permute-start(bf16[2,256,256]{2,1,0:T(8,128)(2,1)} %maximum_select_fusion.8), channel_id=1, source_target_pairs={{0,2},{2,0},{1,3},{3,1},{4,6},{6,4},{5,7},{7,5},{8,10},{10,8},{9,1... | collective-permute-start | bytes 786440 | tf_op jit(solution)/shard_map/ppermute | solution.py:18
  58.4 14.8 %collective-permute-start.5 = (bf16[2,512,256]{2,1,0:T(8,128)(2,1)S(1)}, bf16[2,512,256]{2,1,0:T(8,128)(2,1)}, u32[]{:S(2)}, u32[]{:S(2)}) collective-permute-start(bf16[2,512,256]{2,1,0:T(8,128)(2,1)S(1)} %maximum_select_fusion.4), channel_id=1, source_target_pairs={{0,4},{4,0},{1,5},{5,1},{2,6},{6,2},{3,7},{7,3},{8,12},{12,8},{9,1... | collective-permute-start | bytes 1572872 | tf_op jit(solution)/shard_map/ppermute | solution.py:18
  62.3 12.3 %copy-start.19 = (bf16[2,1,16384]{2,0,1:T(2,128)(2,1)S(1)}, bf16[2,1,16384]{2,0,1:T(2,128)(2,1)}, u32[]{:S(2)}) copy-start(bf16[2,1,16384]{2,0,1:T(2,128)(2,1)} %copy.384) | copy-start | bytes 196612
  62.3 12.3 %copy-start.27 = (f32[1,2,8,128]{3,1,2,0:T(2,128)S(1)}, f32[1,2,8,128]{3,1,2,0:T(2,128)}, u32[]{:S(2)}) copy-start(f32[1,2,8,128]{3,1,2,0:T(2,128)} %copy.393) | copy-start | bytes 24580
  62.3 12.3 %copy-start.50 = (f32[2]{0:T(128)S(1)}, f32[2]{0:T(128)}, u32[]{:S(2)}) copy-start(f32[2]{0:T(128)} %copy-done.49) | copy-start | bytes 28
  62.4 12.3 %copy-start.60 = (f32[2,1,128]{2,1,0:T(1,128)S(1)}, f32[2,1,128]{2,1,0:T(1,128)}, u32[]{:S(2)}) copy-start(f32[2,1,128]{2,1,0:T(1,128)} %fusion.177) | copy-start | bytes 3076
  63.1 36.2 %collective-permute-start.11 = (bf16[2,256,256]{2,1,0:T(8,128)(2,1)}, bf16[2,256,256]{2,1,0:T(8,128)(2,1)}, u32[]{:S(2)}, u32[]{:S(2)}) collective-permute-start(bf16[2,256,256]{2,1,0:T(8,128)(2,1)} %fusion.49), channel_id=1, source_target_pairs={{0,2},{2,0},{1,3},{3,1},{4,6},{6,4},{5,7},{7,5},{8,10},{10,8},{9,1... | collective-permute-start | bytes 786440 | tf_op jit(solution)/shard_map/ppermute | solution.py:18
  68.3 23.8 %collective-permute-start.8 = (bf16[2,512,256]{2,1,0:T(8,128)(2,1)}, bf16[2,512,256]{2,1,0:T(8,128)(2,1)}, u32[]{:S(2)}, u32[]{:S(2)}) collective-permute-start(bf16[2,512,256]{2,1,0:T(8,128)(2,1)} %maximum_select_fusion.5), channel_id=1, source_target_pairs={{0,4},{4,0},{1,5},{5,1},{2,6},{6,2},{3,7},{7,3},{8,12},{12,8},{9,1... | collective-permute-start | bytes 1572872 | tf_op jit(solution)/shard_map/ppermute | solution.py:18
  89.2 8.3 %copy-start.6 = (f32[2,256,256]{2,1,0:T(8,128)S(1)}, f32[2,256,256]{2,1,0:T(8,128)}, u32[]{:S(2)}) copy-start(f32[2,256,256]{2,1,0:T(8,128)} %copy-done.5) | copy-start | bytes 1572868
  89.4 15.5 %collective-permute-start.13 = (bf16[2,512,256]{2,1,0:T(8,128)(2,1)S(1)}, bf16[2,512,256]{2,1,0:T(8,128)(2,1)S(1)}, u32[]{:S(2)}, u32[]{:S(2)}) collective-permute-start(bf16[2,512,256]{2,1,0:T(8,128)(2,1)S(1)} %fusion.42), channel_id=1, source_target_pairs={{0,4},{4,0},{1,5},{5,1},{2,6},{6,2},{3,7},{7,3},{8,12},{12,8},{9,1... | collective-permute-start | bytes 1572872 | tf_op jit(solution)/shard_map/ppermute | solution.py:18
  93.8 29.7 %collective-permute-start.9 = (bf16[2,1024,256]{2,1,0:T(8,128)(2,1)S(1)}, bf16[2,1024,256]{2,1,0:T(8,128)(2,1)S(1)}, u32[]{:S(2)}, u32[]{:S(2)}) collective-permute-start(bf16[2,1024,256]{2,1,0:T(8,128)(2,1)S(1)} %maximum_select_fusion.2), channel_id=1, source_target_pairs={{0,8},{8,0},{1,9},{9,1},{2,10},{10,2},{3,11},{11,3},{4,12},{12,4},... | collective-permute-start | bytes 3145736 | tf_op jit(solution)/shard_map/ppermute | solution.py:18
  101.1 60.6 %collective-permute-start.12 = (bf16[2,128,256]{2,1,0:T(8,128)(2,1)}, bf16[2,128,256]{2,1,0:T(8,128)(2,1)}, u32[]{:S(2)}, u32[]{:S(2)}) collective-permute-start(bf16[2,128,256]{2,1,0:T(8,128)(2,1)} %fusion.68), channel_id=1, source_target_pairs={{0,1},{1,0},{2,3},{3,2},{4,5},{5,4},{6,7},{7,6},{8,9},{9,8},{10,11... | collective-permute-start | bytes 393224 | tf_op jit(solution)/shard_map/ppermute | solution.py:18
  105.1 19.0 %copy-start.18 = (bf16[2,1,16384]{2,0,1:T(2,128)(2,1)S(1)}, bf16[2,1,16384]{2,0,1:T(2,128)(2,1)}, u32[]{:S(2)}) copy-start(bf16[2,1,16384]{2,0,1:T(2,128)(2,1)} %copy.388) | copy-start | bytes 196612
  105.1 19.0 %copy-start.48 = (f32[2]{0:T(128)S(1)}, f32[2]{0:T(128)}, u32[]{:S(2)}) copy-start(f32[2]{0:T(128)} %copy-done.47) | copy-start | bytes 28
  105.2 19.0 %copy-start.59 = (f32[2,1,128]{2,1,0:T(1,128)S(1)}, f32[2,1,128]{2,1,0:T(1,128)}, u32[]{:S(2)}) copy-start(f32[2,1,128]{2,1,0:T(1,128)} %fusion.167) | copy-start | bytes 3076
  156.2 5.5 %copy-start.8 = (f32[2,256,256]{2,1,0:T(8,128)S(1)}, f32[2,256,256]{2,1,0:T(8,128)}, u32[]{:S(2)}) copy-start(f32[2,256,256]{2,1,0:T(8,128)} %copy-done.7) | copy-start | bytes 1572868
  158.1 24.7 %collective-permute-start.16 = (bf16[2,1024,256]{2,1,0:T(8,128)(2,1)S(1)}, bf16[2,1024,256]{2,1,0:T(8,128)(2,1)S(1)}, u32[]{:S(2)}, u32[]{:S(2)}) collective-permute-start(bf16[2,1024,256]{2,1,0:T(8,128)(2,1)S(1)} %fusion.36), channel_id=1, source_target_pairs={{0,8},{8,0},{1,9},{9,1},{2,10},{10,2},{3,11},{11,3},{4,12},{12,4},... | collective-permute-start | bytes 3145736 | tf_op jit(solution)/shard_map/ppermute | solution.py:18
  158.3 8.7 %collective-permute-start.14 = (bf16[2,256,256]{2,1,0:T(8,128)(2,1)S(1)}, bf16[2,256,256]{2,1,0:T(8,128)(2,1)S(1)}, u32[]{:S(2)}, u32[]{:S(2)}) collective-permute-start(bf16[2,256,256]{2,1,0:T(8,128)(2,1)S(1)} %fusion.50), channel_id=1, source_target_pairs={{0,2},{2,0},{1,3},{3,1},{4,6},{6,4},{5,7},{7,5},{8,10},{10,8},{9,1... | collective-permute-start | bytes 786440 | tf_op jit(solution)/shard_map/ppermute | solution.py:18
  161.6 21.2 %copy-start = (f32[2,1,1024,256]{3,2,0,1:T(8,128)S(1)}, f32[2,1,1024,256]{3,2,0,1:T(8,128)}, u32[]{:S(2)}) copy-start(f32[2,1,1024,256]{3,2,0,1:T(8,128)} %copy.158) | copy-start | bytes 6291460
  167.1 16.3 %copy-start.12 = (bf16[2,1024,256]{2,1,0:T(8,128)(2,1)S(1)}, bf16[2,1024,256]{2,1,0:T(8,128)(2,1)}, u32[]{:S(2)}) copy-start(bf16[2,1024,256]{2,1,0:T(8,128)(2,1)} %copy-done.11) | copy-start | bytes 3145732
  167.1 16.3 %copy-start.16 = (bf16[2,128,1024]{2,1,0:T(8,128)(2,1)S(1)}, bf16[2,128,1024]{2,1,0:T(8,128)(2,1)}, u32[]{:S(2)}) copy-start(bf16[2,128,1024]{2,1,0:T(8,128)(2,1)} %copy-done.15) | copy-start | bytes 1572868
  167.1 16.7 %collective-permute-start.15 = (bf16[2,128,256]{2,1,0:T(8,128)(2,1)S(1)}, bf16[2,128,256]{2,1,0:T(8,128)(2,1)S(1)}, u32[]{:S(2)}, u32[]{:S(2)}) collective-permute-start(bf16[2,128,256]{2,1,0:T(8,128)(2,1)S(1)} %fusion.69), channel_id=1, source_target_pairs={{0,1},{1,0},{2,3},{3,2},{4,5},{5,4},{6,7},{7,6},{8,9},{9,8},{10,11... | collective-permute-start | bytes 393224 | tf_op jit(solution)/shard_map/ppermute | solution.py:18
  183.3 9.3 %collective-permute-start.17 = (bf16[2,512,256]{2,1,0:T(8,128)(2,1)S(1)}, bf16[2,512,256]{2,1,0:T(8,128)(2,1)S(1)}, u32[]{:S(2)}, u32[]{:S(2)}) collective-permute-start(bf16[2,512,256]{2,1,0:T(8,128)(2,1)S(1)} %fusion.43), channel_id=1, source_target_pairs={{0,4},{4,0},{1,5},{5,1},{2,6},{6,2},{3,7},{7,3},{8,12},{12,8},{9,1... | collective-permute-start | bytes 1572872 | tf_op jit(solution)/shard_map/ppermute | solution.py:18
  185.6 11.5 %copy-start.20 = (f32[2,2,16384]{2,1,0:T(2,128)S(1)}, f32[2,2,16384]{2,1,0:T(2,128)}, u32[]{:S(2)}) copy-start(f32[2,2,16384]{2,1,0:T(2,128)} %reshape_reshape_transpose.2) | copy-start | bytes 786436
  185.6 11.5 %copy-start.26 = (f32[1,2,128,128]{3,1,2,0:T(2,128)S(1)}, f32[1,2,128,128]{3,1,2,0:T(2,128)}, u32[]{:S(2)}) copy-start(f32[1,2,128,128]{3,1,2,0:T(2,128)} %copy.373) | copy-start | bytes 393220
  185.6 11.4 %copy-start.52 = (f32[2,2]{1,0:T(2,128)S(1)}, f32[2,2]{1,0:T(2,128)}, u32[]{:S(2)}) copy-start(f32[2,2]{1,0:T(2,128)} %copy-done.51) | copy-start | bytes 52
  185.6 11.4 %copy-start.53 = (f32[2,2]{1,0:T(2,128)S(1)}, f32[2,2]{1,0:T(2,128)}, u32[]{:S(2)}) copy-start(f32[2,2]{1,0:T(2,128)} %get-tuple-element.207) | copy-start | bytes 52
  185.6 11.4 %copy-start.54 = (f32[2,2]{1,0:T(2,128)S(1)}, f32[2,2]{1,0:T(2,128)}, u32[]{:S(2)}) copy-start(f32[2,2]{1,0:T(2,128)} %get-tuple-element.208) | copy-start | bytes 52
  185.6 11.4 %copy-start.55 = (f32[2,2]{1,0:T(2,128)S(1)}, f32[2,2]{1,0:T(2,128)}, u32[]{:S(2)}) copy-start(f32[2,2]{1,0:T(2,128)} %get-tuple-element.203) | copy-start | bytes 52
  185.6 11.4 %copy-start.56 = (f32[2,2]{1,0:T(2,128)S(1)}, f32[2,2]{1,0:T(2,128)}, u32[]{:S(2)}) copy-start(f32[2,2]{1,0:T(2,128)} %get-tuple-element.204) | copy-start | bytes 52
  185.6 11.4 %copy-start.58 = (s32[2,2]{1,0:T(2,128)S(1)}, s32[2,2]{1,0:T(2,128)}, u32[]{:S(2)}) copy-start(s32[2,2]{1,0:T(2,128)} %copy-done.57) | copy-start | bytes 52
  193.5 68.7 %collective-permute-start.18 = (bf16[2,256,256]{2,1,0:T(8,128)(2,1)}, bf16[2,256,256]{2,1,0:T(8,128)(2,1)S(1)}, u32[]{:S(2)}, u32[]{:S(2)}) collective-permute-start(bf16[2,256,256]{2,1,0:T(8,128)(2,1)} %fusion.51), channel_id=1, source_target_pairs={{0,2},{2,0},{1,3},{3,1},{4,6},{6,4},{5,7},{7,5},{8,10},{10,8},{9,1... | collective-permute-start | bytes 786440 | tf_op jit(solution)/shard_map/ppermute | solution.py:18
  198.3 65.4 %copy-start.37 = (f32[256]{0:T(256)S(1)}, f32[256]{0:T(256)}, u32[]{:S(2)}) copy-start(f32[256]{0:T(256)} %param.13) | copy-start | bytes 3076
  199.1 68.8 %copy-start.17 = (f32[2,2,32768]{2,1,0:T(2,128)S(1)}, f32[2,2,32768]{2,1,0:T(2,128)}, u32[]{:S(2)}) copy-start(f32[2,2,32768]{2,1,0:T(2,128)} %reshape.1667) | copy-start | bytes 1572868
  199.1 68.8 %copy-start.21 = (f32[1,2,128,256]{3,1,2,0:T(2,128)S(1)}, f32[1,2,128,256]{3,1,2,0:T(2,128)}, u32[]{:S(2)}) copy-start(f32[1,2,128,256]{3,1,2,0:T(2,128)} %copy.191) | copy-start | bytes 786436
  199.1 68.8 %copy-start.22 = (f32[1,2,128,256]{3,1,2,0:T(2,128)S(1)}, f32[1,2,128,256]{3,1,2,0:T(2,128)}, u32[]{:S(2)}) copy-start(f32[1,2,128,256]{3,1,2,0:T(2,128)} %copy.192) | copy-start | bytes 786436
  262.3 5.3 %collective-permute-start.19 = (bf16[2,128,256]{2,1,0:T(8,128)(2,1)S(1)}, bf16[2,128,256]{2,1,0:T(8,128)(2,1)S(1)}, u32[]{:S(2)}, u32[]{:S(2)}) collective-permute-start(bf16[2,128,256]{2,1,0:T(8,128)(2,1)S(1)} %fusion.70), channel_id=1, source_target_pairs={{0,1},{1,0},{2,3},{3,2},{4,5},{5,4},{6,7},{7,6},{8,9},{9,8},{10,11... | collective-permute-start | bytes 393224 | tf_op jit(solution)/shard_map/ppermute | solution.py:18
  (19 other events, 51.9 us)
where the time goes:
time: 277 us; the launch traced here: 273 us
  waiting for transfers between devices  63.6 us (23%)
  blocking collectives  63 us (23%)
  local copies, waits for them, and re-layouts  59.3 us (21%)
  starting transfers between devices  34.9 us (13%)
  other arithmetic  27.5 us (10%)
  matrix products  21.6 us (8%)
    ppermute x20, waiting for transfers between devices, swapped(): return lax.ppermute(block, axis, route)  63.6 us
    psum x1, blocking collectives, body(): lax.psum(jnp.sum(query_raw.astype(jnp.float32) * dq_rows, axis=0), ('dp',...  63 us
    ppermute x20, starting transfers between devices, swapped(): return lax.ppermute(block, axis, route)  34.9 us
    unnamed x153, local copies, waits for them, and re-layouts  24.8 us
    slice x3, local copies, waits for them, and re-layouts, swap_down(): kept_half = jnp.where(lower_half, halves[:, 0], halves[:, 1])  12.9 us
    reshape x3, local copies, waits for them, and re-layouts, swap_down(): halves = sums_kv.reshape(head_count, 2, -1, sums_kv.shape[-1])  10.3 us
    dot_general x25, matrix products, pick_blocks(): jnp.einsum('hsb,hbx->hsx', table, flat, precision=lax.Precision.HIGHEST,...  10.3 us
    select_n x10, other arithmetic, swap_up(): jnp.where(lower_half, jnp.concatenate([payload, partner], axis=1), jnp.co...  9.27 us
  transfers between devices with their start and end apart: 20, of which 9 were waited for; matrix products, arithmetic and copies ran while one was open for 34% of the time, Pallas kernels for 0%

commit v1 on v0

--- a/solution.py
+++ b/solution.py
@@ -214,7 +214,9 @@
     grad_queries = (dq_rows * q_gain).astype(jnp.bfloat16)
     grad_keys = to_rows(kv_acc[..., :head_dim]).astype(jnp.bfloat16)
     grad_values = to_rows(kv_acc[..., head_dim:]).astype(jnp.bfloat16)
-    gain_total = lax.psum(jnp.sum(query_raw.astype(jnp.float32) * dq_rows, axis=0), ("dp", "ctx"))
+    gain_total = lax.psum(
+        lax.psum(jnp.sum(query_raw.astype(jnp.float32) * dq_rows, axis=0), "ctx"), "dp"
+    )
     return (grad_queries[None], grad_keys[None], grad_values[None], gain_total)
 
 

time: 277 us -> 264 us (0.953)
  blocking collectives: 63 us -> 49.2 us
    psum x1 -> x2, blocking collectives: 63 us -> 49.2 us  [the longest x1 36.2 us: body(): lax.psum(jnp.sum(query_raw.astype(jnp.float32) * dq_rows, axis=0), 'ctx')]
  transfers between devices with their start and end apart: 20 -> 20, of which waited for: 9 -> 9; matrix products, arithmetic and copies ran while one was open for 34% -> 36% of each run, Pallas kernels for 0% -> 0%
where the time goes in v1:
time: 264 us; the launch traced here: 259 us
  waiting for transfers between devices  63.5 us (24%)
  local copies, waits for them, and re-layouts  58.9 us (22%)
  blocking collectives  49.2 us (19%)
  starting transfers between devices  35.5 us (13%)
  other arithmetic  27.6 us (10%)
  matrix products  21.7 us (8%)
    ppermute x20, waiting for transfers between devices, swapped(): return lax.ppermute(block, axis, route)  63.5 us
    psum x1, blocking collectives, body(): lax.psum(jnp.sum(query_raw.astype(jnp.float32) * dq_rows, axis=0), 'ctx')  36.2 us
    ppermute x20, starting transfers between devices, swapped(): return lax.ppermute(block, axis, route)  35.5 us
    unnamed x153, local copies, waits for them, and re-layouts  24.5 us
    psum x1, blocking collectives, body(): lax.psum(lax.psum(jnp.sum(query_raw.astype(jnp.float32) * dq_rows, axis=0...  13 us
    slice x3, local copies, waits for them, and re-layouts, swap_down(): kept_half = jnp.where(lower_half, halves[:, 0], halves[:, 1])  12.9 us
    dot_general x25, matrix products, pick_blocks(): jnp.einsum('hsb,hbx->hsx', table, flat, precision=lax.Precision.HIGHEST,...  10.3 us
    reshape x3, local copies, waits for them, and re-layouts, swap_down(): halves = sums_kv.reshape(head_count, 2, -1, sums_kv.shape[-1])  10.3 us
  transfers between devices with their start and end apart: 20, of which 9 were waited for; matrix products, arithmetic and copies ran while one was open for 36% of the time, Pallas kernels for 0%

profile of v1, /device:TPU:0, one launch (start us, length us, event | category | flops | bytes accessed | tf_op | source)
XLA Modules:
  0.0 259.1 jit_solution(16658535741942920779)
XLA Ops:
  0.7 0.9 reshape_squeeze.12
  1.7 1.7 clamp_reduce_fusion.3
  4.0 0.9 reshape_squeeze.15
  5.4 1.7 collective-permute-start
  9.4 1.7 collective-permute-start.3
  11.9 1.1 collective-permute-start.6
  19.4 0.9 fusion.193
  20.4 0.9 fusion.203
  26.9 1.0 copy.380
  28.1 0.9 reshape_reshape_transpose.2
  29.0 1.2 reshape.1667
  33.1 0.8 copy-done.5
  34.7 3.2 %collective-permute-start.2 = (bf16[2,256,256]{2,1,0:T(8,128)(2,1)S(1)}, bf16[2,256,256]{2,1,0:T(8,128)(2,1)S(1)}, u32[]{:S(2)}, u32[]{:S(2)}) collective-permute-start(bf16[2,256,256]{2,1,0:T(8,128)(2,1)S(1)} %maximum_select_fusion.7), channel_id=1, source_target_pairs={{0,2},{2,0},{1,3},{3,1},{4,6},{6,4},{5,7},{7,5},{8,10},{10,8},{9,1... | collective-permute-start | bytes 786440 | tf_op jit(solution)/shard_map/ppermute | solution.py:18
  38.1 0.8 copy.373
  39.5 0.8 maximum_select_fusion.9
  40.3 2.0 collective-permute-start.7
  42.3 0.8 maximum_select_fusion.8
  43.1 1.5 collective-permute-start.4
  44.6 1.0 collective-permute-done.2
  48.1 9.2 %collective-permute-done.4 = bf16[2,256,256]{2,1,0:T(8,128)(2,1)} collective-permute-done((bf16[2,256,256]{2,1,0:T(8,128)(2,1)}, bf16[2,256,256]{2,1,0:T(8,128)(2,1)}, u32[]{:S(2)}, u32[]{:S(2)}) %collective-permute-start.4) | collective-permute-done | bytes 262176 | tf_op jit(solution)/shard_map/ppermute | solution.py:18
  57.3 1.3 maximum_select_fusion.4
  58.6 2.4 collective-permute-start.5
  61.0 0.8 fusion.213
  62.5 0.8 fusion.49
  63.3 3.0 %collective-permute-start.11 = (bf16[2,256,256]{2,1,0:T(8,128)(2,1)}, bf16[2,256,256]{2,1,0:T(8,128)(2,1)}, u32[]{:S(2)}, u32[]{:S(2)}) collective-permute-start(bf16[2,256,256]{2,1,0:T(8,128)(2,1)} %fusion.49), channel_id=1, source_target_pairs={{0,2},{2,0},{1,3},{3,1},{4,6},{6,4},{5,7},{7,5},{8,10},{10,8},{9,1... | collective-permute-start | bytes 786440 | tf_op jit(solution)/shard_map/ppermute | solution.py:18
  66.3 2.1 maximum_select_fusion.5
  68.6 4.8 %collective-permute-done.5 = bf16[2,512,256]{2,1,0:T(8,128)(2,1)} collective-permute-done((bf16[2,512,256]{2,1,0:T(8,128)(2,1)S(1)}, bf16[2,512,256]{2,1,0:T(8,128)(2,1)}, u32[]{:S(2)}, u32[]{:S(2)}) %collective-permute-start.5) | collective-permute-done | bytes 524320 | tf_op jit(solution)/shard_map/ppermute | solution.py:18
  73.3 1.4 maximum_select_fusion.1
  77.2 1.5 pad_maximum_fusion.1
  78.7 3.0 %reshape.1673 = f32[2,2,512,256]{2,1,3,0:T(2,128)S(1)} reshape(f32[2,1024,256]{1,2,0:T(8,128)} %pad_maximum_fusion.1) | data formatting | bytes 4194304 | tf_op jit(solution)/shard_map/reshape | solution.py:137
  81.7 3.0 %fusion.212 = (f32[2,1,512,256]{2,1,3,0:T(1,128)}, f32[2,1,512,256]{2,1,3,0:T(1,128)}) fusion(f32[2,2,512,256]{2,1,3,0:T(2,128)S(1)} %reshape.1673), kind=kLoop, calls=%fused_computation.413 | loop fusion | bytes 4194304 | tf_op jit(solution)/shard_map/slice | solution.py:139
  84.7 2.3 copy.151
  87.1 2.4 copy.152
  89.6 2.7 %collective-permute-start.13 = (bf16[2,512,256]{2,1,0:T(8,128)(2,1)S(1)}, bf16[2,512,256]{2,1,0:T(8,128)(2,1)S(1)}, u32[]{:S(2)}, u32[]{:S(2)}) collective-permute-start(bf16[2,512,256]{2,1,0:T(8,128)(2,1)S(1)} %fusion.42), channel_id=1, source_target_pairs={{0,4},{4,0},{1,5},{5,1},{2,6},{6,2},{3,7},{7,3},{8,12},{12,8},{9,1... | collective-permute-start | bytes 1572872 | tf_op jit(solution)/shard_map/ppermute | solution.py:18
  92.3 1.8 maximum_select_fusion.2
  94.0 3.7 %collective-permute-start.9 = (bf16[2,1024,256]{2,1,0:T(8,128)(2,1)S(1)}, bf16[2,1024,256]{2,1,0:T(8,128)(2,1)S(1)}, u32[]{:S(2)}, u32[]{:S(2)}) collective-permute-start(bf16[2,1024,256]{2,1,0:T(8,128)(2,1)S(1)} %maximum_select_fusion.2), channel_id=1, source_target_pairs={{0,8},{8,0},{1,9},{9,1},{2,10},{10,2},{3,11},{11,3},{4,12},{12,4},... | collective-permute-start | bytes 3145736 | tf_op jit(solution)/shard_map/ppermute | solution.py:18
  97.7 1.0 fusion.58
  98.7 0.9 copy.191
  99.6 1.0 bitcast_add_fusion.5
  100.6 0.8 fusion.68
  101.4 1.7 collective-permute-start.12
  103.1 2.0 collective-permute-done.13
  105.4 18.4 %collective-permute-done.9 = bf16[2,1024,256]{2,1,0:T(8,128)(2,1)S(1)} collective-permute-done((bf16[2,1024,256]{2,1,0:T(8,128)(2,1)S(1)}, bf16[2,1024,256]{2,1,0:T(8,128)(2,1)S(1)}, u32[]{:S(2)}, u32[]{:S(2)}) %collective-permute-start.9) | collective-permute-done | bytes 1048608 | tf_op jit(solution)/shard_map/ppermute | solution.py:18
  127.6 2.5 pad_maximum_fusion
  130.1 6.6 %reshape.1677 = f32[2,2,1024,256]{2,1,3,0:T(2,128)} reshape(f32[2,2048,256]{1,2,0:T(8,128)} %pad_maximum_fusion) | data formatting | bytes 8388608 | tf_op jit(solution)/shard_map/reshape | solution.py:137
  136.7 9.1 %fusion.211 = (f32[2,1,1024,256]{2,1,3,0:T(1,128)}, f32[2,1,1024,256]{2,1,3,0:T(1,128)}) fusion(f32[2,2,1024,256]{2,1,3,0:T(2,128)} %reshape.1677), kind=kLoop, calls=%fused_computation.412 | loop fusion | bytes 8388608 | tf_op jit(solution)/shard_map/slice | solution.py:139
  145.8 4.6 %copy.157 = f32[2,1,1024,256]{3,2,0,1:T(8,128)S(1)} copy(f32[2,1,1024,256]{2,1,3,0:T(1,128)} %get-tuple-element.141) | data formatting | bytes 4194304
  150.4 6.1 %copy.158 = f32[2,1,1024,256]{3,2,0,1:T(8,128)} copy(f32[2,1,1024,256]{2,1,3,0:T(1,128)} %get-tuple-element.142) | data formatting | bytes 4194304
  156.4 1.9 fusion.36
  158.5 3.1 %collective-permute-start.14 = (bf16[2,256,256]{2,1,0:T(8,128)(2,1)S(1)}, bf16[2,256,256]{2,1,0:T(8,128)(2,1)S(1)}, u32[]{:S(2)}, u32[]{:S(2)}) collective-permute-start(bf16[2,256,256]{2,1,0:T(8,128)(2,1)S(1)} %fusion.50), channel_id=1, source_target_pairs={{0,2},{2,0},{1,3},{3,1},{4,6},{6,4},{5,7},{7,5},{8,10},{10,8},{9,1... | collective-permute-start | bytes 786440 | tf_op jit(solution)/shard_map/ppermute | solution.py:18
  162.0 1.1 fusion.55
  163.0 0.9 copy.192
  164.0 3.3 %collective-permute-done.14 = bf16[2,256,256]{2,1,0:T(8,128)(2,1)S(1)} collective-permute-done((bf16[2,256,256]{2,1,0:T(8,128)(2,1)S(1)}, bf16[2,256,256]{2,1,0:T(8,128)(2,1)S(1)}, u32[]{:S(2)}, u32[]{:S(2)}) %collective-permute-start.14) | collective-permute-done | bytes 262176 | tf_op jit(solution)/shard_map/ppermute | solution.py:18
  167.4 0.8 collective-permute-start.15
  168.2 14.6 %collective-permute-done.16 = bf16[2,1024,256]{2,1,0:T(8,128)(2,1)S(1)} collective-permute-done((bf16[2,1024,256]{2,1,0:T(8,128)(2,1)S(1)}, bf16[2,1024,256]{2,1,0:T(8,128)(2,1)S(1)}, u32[]{:S(2)}, u32[]{:S(2)}) %collective-permute-start.16) | collective-permute-done | bytes 1048608 | tf_op jit(solution)/shard_map/ppermute | solution.py:18
  185.7 6.9 %collective-permute-done.17 = bf16[2,512,256]{2,1,0:T(8,128)(2,1)S(1)} collective-permute-done((bf16[2,512,256]{2,1,0:T(8,128)(2,1)S(1)}, bf16[2,512,256]{2,1,0:T(8,128)(2,1)S(1)}, u32[]{:S(2)}, u32[]{:S(2)}) %collective-permute-start.17) | collective-permute-done | bytes 524320 | tf_op jit(solution)/shard_map/ppermute | solution.py:18
  192.8 0.7 fusion.51
  193.5 3.8 %collective-permute-start.18 = (bf16[2,256,256]{2,1,0:T(8,128)(2,1)}, bf16[2,256,256]{2,1,0:T(8,128)(2,1)S(1)}, u32[]{:S(2)}, u32[]{:S(2)}) collective-permute-start(bf16[2,256,256]{2,1,0:T(8,128)(2,1)} %fusion.51), channel_id=1, source_target_pairs={{0,2},{2,0},{1,3},{3,1},{4,6},{6,4},{5,7},{7,5},{8,10},{10,8},{9,1... | collective-permute-start | bytes 786440 | tf_op jit(solution)/shard_map/ppermute | solution.py:18
  197.3 1.2 fusion.6
  199.4 36.2 %psum.14 = f32[256]{0:T(256)S(1)} all-reduce(f32[256]{0:T(256)S(1)} %bitcast.569), channel_id=1, replica_groups=mesh['dp'=8,'ctx'=16] {'ctx'}, use_global_device_ids=true, to_apply=%region_1.2 | all-reduce | flops 256 | bytes 2048 | tf_op jit(solution)/shard_map/psum | solution.py:218
  235.6 13.0 %psum.15 = f32[256]{0:T(256)} all-reduce(f32[256]{0:T(256)S(1)} %psum.14), channel_id=1, replica_groups=mesh['dp'=8,'ctx'=16] {'dp'}, use_global_device_ids=true, to_apply=%region_2.3 | all-reduce | flops 256 | bytes 2048 | tf_op jit(solution)/shard_map/psum | solution.py:217
  248.7 1.5 collective-permute-start.19
  250.8 3.4 %collective-permute-done.19 = bf16[2,128,256]{2,1,0:T(8,128)(2,1)S(1)} collective-permute-done((bf16[2,128,256]{2,1,0:T(8,128)(2,1)S(1)}, bf16[2,128,256]{2,1,0:T(8,128)(2,1)S(1)}, u32[]{:S(2)}, u32[]{:S(2)}) %collective-permute-start.19) | collective-permute-done | bytes 131104 | tf_op jit(solution)/shard_map/ppermute | solution.py:18
  254.5 2.4 fusion.3
  (297 shorter events, 37.3 us)
Async XLA Ops:
  3.4 5.4 %copy-start.28 = (s32[2]{0:T(128)}, s32[2]{0:T(128)S(1)}, u32[]{:S(2)}) copy-start(s32[2]{0:T(128)S(1)} %get-tuple-element.178) | copy-start | bytes 28
  3.4 5.4 %copy-start.30 = (s32[2]{0:T(128)}, s32[2]{0:T(128)S(1)}, u32[]{:S(2)}) copy-start(s32[2]{0:T(128)S(1)} %get-tuple-element.181) | copy-start | bytes 28
  3.4 5.4 %copy-start.32 = (s32[2]{0:T(128)}, s32[2]{0:T(128)S(1)}, u32[]{:S(2)}) copy-start(s32[2]{0:T(128)S(1)} %get-tuple-element.118) | copy-start | bytes 28
  3.4 5.4 %copy-start.34 = (s32[2]{0:T(128)}, s32[2]{0:T(128)S(1)}, u32[]{:S(2)}) copy-start(s32[2]{0:T(128)S(1)} %get-tuple-element.164) | copy-start | bytes 28
  5.4 26.6 %collective-permute-start = (bf16[2,128,256]{2,1,0:T(8,128)(2,1)S(1)}, bf16[2,128,256]{2,1,0:T(8,128)(2,1)S(1)}, u32[]{:S(2)}, u32[]{:S(2)}) collective-permute-start(bf16[2,128,256]{2,1,0:T(8,128)(2,1)S(1)} %bitcast_dynamic-update-slice_fusion.6), channel_id=1, source_target_pairs={{0,1},{1,0},{2,3},{3,2},{4,5},{5,4},{6,7},{7,6},{8,9},{9,8},{10,11... | collective-permute-start | bytes 393224 | tf_op jit(solution)/shard_map/ppermute | solution.py:18
  7.6 5.4 %copy-start.46 = (f32[1,2,256]{2,1,0:T(2,128)S(1)}, f32[1,2,256]{2,1,0:T(2,128)}, u32[]{:S(2)}) copy-start(f32[1,2,256]{2,1,0:T(2,128)} %param.11) | copy-start | bytes 6148
  7.9 26.7 %collective-permute-start.1 = (bf16[2,128,256]{2,1,0:T(8,128)(2,1)S(1)}, bf16[2,128,256]{2,1,0:T(8,128)(2,1)S(1)}, u32[]{:S(2)}, u32[]{:S(2)}) collective-permute-start(bf16[2,128,256]{2,1,0:T(8,128)(2,1)S(1)} %bitcast_dynamic-update-slice_fusion.4), channel_id=1, source_target_pairs={{0,1},{1,0},{2,3},{3,2},{4,5},{5,4},{6,7},{7,6},{8,9},{9,8},{10,11... | collective-permute-start | bytes 393224 | tf_op jit(solution)/shard_map/ppermute | solution.py:18
  8.5 8.4 %copy-start.25 = (bf16[1,256,256]{2,1,0:T(8,128)(2,1)S(1)}, bf16[1,256,256]{2,1,0:T(8,128)(2,1)}, u32[]{:S(2)}) copy-start(bf16[1,256,256]{2,1,0:T(8,128)(2,1)} %param.10) | copy-start | bytes 393220
  9.4 32.8 %collective-permute-start.3 = (bf16[2,128,256]{2,1,0:T(8,128)(2,1)S(1)}, bf16[2,128,256]{2,1,0:T(8,128)(2,1)S(1)}, u32[]{:S(2)}, u32[]{:S(2)}) collective-permute-start(bf16[2,128,256]{2,1,0:T(8,128)(2,1)S(1)} %bitcast_dynamic-update-slice_fusion.2), channel_id=1, source_target_pairs={{0,1},{1,0},{2,3},{3,2},{4,5},{5,4},{6,7},{7,6},{8,9},{9,8},{10,11... | collective-permute-start | bytes 393224 | tf_op jit(solution)/shard_map/ppermute | solution.py:18
  11.9 27.5 %collective-permute-start.6 = (bf16[2,128,256]{2,1,0:T(8,128)(2,1)S(1)}, bf16[2,128,256]{2,1,0:T(8,128)(2,1)S(1)}, u32[]{:S(2)}, u32[]{:S(2)}) collective-permute-start(bf16[2,128,256]{2,1,0:T(8,128)(2,1)S(1)} %bitcast_dynamic-update-slice_fusion), channel_id=1, source_target_pairs={{0,1},{1,0},{2,3},{3,2},{4,5},{5,4},{6,7},{7,6},{8,9},{9,8},{10,11... | collective-permute-start | bytes 393224 | tf_op jit(solution)/shard_map/ppermute | solution.py:18
  13.0 8.3 %copy-start.57 = (s32[2,2]{1,0:T(2,128)}, s32[2,2]{1,0:T(2,128)S(1)}, u32[]{:S(2)}) copy-start(s32[2,2]{1,0:T(2,128)S(1)} %iota_clamp_fusion) | copy-start | bytes 52
  13.1 8.6 %copy-start.51 = (f32[2,2]{1,0:T(2,128)}, f32[2,2]{1,0:T(2,128)S(1)}, u32[]{:S(2)}) copy-start(f32[2,2]{1,0:T(2,128)S(1)} %and_convert_fusion.8) | copy-start | bytes 52
  24.9 5.4 %copy-start.42 = (s32[2,1]{1,0:T(2,128)S(1)}, s32[2,1]{1,0:T(2,128)}, u32[]{:S(2)}) copy-start(s32[2,1]{1,0:T(2,128)} %get-tuple-element.179) | copy-start | bytes 28
  24.9 5.4 %copy-start.43 = (s32[2,1]{1,0:T(2,128)S(1)}, s32[2,1]{1,0:T(2,128)}, u32[]{:S(2)}) copy-start(s32[2,1]{1,0:T(2,128)} %get-tuple-element.180) | copy-start | bytes 28
  24.9 5.5 %copy-start.40 = (s32[2,1]{1,0:T(2,128)S(1)}, s32[2,1]{1,0:T(2,128)}, u32[]{:S(2)}) copy-start(s32[2,1]{1,0:T(2,128)} %get-tuple-element.176) | copy-start | bytes 28
  24.9 5.5 %copy-start.41 = (s32[2,1]{1,0:T(2,128)S(1)}, s32[2,1]{1,0:T(2,128)}, u32[]{:S(2)}) copy-start(s32[2,1]{1,0:T(2,128)} %get-tuple-element.177) | copy-start | bytes 28
  24.9 5.6 %copy-start.38 = (s32[2,1]{1,0:T(2,128)S(1)}, s32[2,1]{1,0:T(2,128)}, u32[]{:S(2)}) copy-start(s32[2,1]{1,0:T(2,128)} %get-tuple-element.119) | copy-start | bytes 28
  25.0 5.6 %copy-start.39 = (s32[2,1]{1,0:T(2,128)S(1)}, s32[2,1]{1,0:T(2,128)}, u32[]{:S(2)}) copy-start(s32[2,1]{1,0:T(2,128)} %get-tuple-element.120) | copy-start | bytes 28
  25.0 5.7 %copy-start.33 = (s32[2]{0:T(128)S(1)}, s32[2]{0:T(128)}, u32[]{:S(2)}) copy-start(s32[2]{0:T(128)} %copy-done.32) | copy-start | bytes 28
  25.0 5.7 %copy-start.35 = (s32[2]{0:T(128)S(1)}, s32[2]{0:T(128)}, u32[]{:S(2)}) copy-start(s32[2]{0:T(128)} %copy-done.34) | copy-start | bytes 28
  25.0 6.4 %copy-start.29 = (s32[2]{0:T(128)S(1)}, s32[2]{0:T(128)}, u32[]{:S(2)}) copy-start(s32[2]{0:T(128)} %copy-done.28) | copy-start | bytes 28
  25.0 6.4 %copy-start.31 = (s32[2]{0:T(128)S(1)}, s32[2]{0:T(128)}, u32[]{:S(2)}) copy-start(s32[2]{0:T(128)} %copy-done.30) | copy-start | bytes 28
  25.3 6.8 %copy-start.62 = (f32[2,1,128]{2,1,0:T(1,128)S(1)}, f32[2,1,128]{2,1,0:T(1,128)}, u32[]{:S(2)}) copy-start(f32[2,1,128]{2,1,0:T(1,128)} %fusion.197) | copy-start | bytes 3076
  33.1 12.7 %copy-start.61 = (f32[2,1,128]{2,1,0:T(1,128)S(1)}, f32[2,1,128]{2,1,0:T(1,128)}, u32[]{:S(2)}) copy-start(f32[2,1,128]{2,1,0:T(1,128)} %fusion.187) | copy-start | bytes 3076
  34.7 10.9 %collective-permute-start.2 = (bf16[2,256,256]{2,1,0:T(8,128)(2,1)S(1)}, bf16[2,256,256]{2,1,0:T(8,128)(2,1)S(1)}, u32[]{:S(2)}, u32[]{:S(2)}) collective-permute-start(bf16[2,256,256]{2,1,0:T(8,128)(2,1)S(1)} %maximum_select_fusion.7), channel_id=1, source_target_pairs={{0,2},{2,0},{1,3},{3,1},{4,6},{6,4},{5,7},{7,5},{8,10},{10,8},{9,1... | collective-permute-start | bytes 786440 | tf_op jit(solution)/shard_map/ppermute | solution.py:18
  38.9 58.9 %collective-permute-start.10 = (bf16[2,128,256]{2,1,0:T(8,128)(2,1)}, bf16[2,128,256]{2,1,0:T(8,128)(2,1)}, u32[]{:S(2)}, u32[]{:S(2)}) collective-permute-start(bf16[2,128,256]{2,1,0:T(8,128)(2,1)} %fusion.67), channel_id=1, source_target_pairs={{0,1},{1,0},{2,3},{3,2},{4,5},{5,4},{6,7},{7,6},{8,9},{9,8},{10,11... | collective-permute-start | bytes 393224 | tf_op jit(solution)/shard_map/ppermute | solution.py:18
  40.3 26.1 %collective-permute-start.7 = (bf16[2,256,256]{2,1,0:T(8,128)(2,1)}, bf16[2,256,256]{2,1,0:T(8,128)(2,1)}, u32[]{:S(2)}, u32[]{:S(2)}) collective-permute-start(bf16[2,256,256]{2,1,0:T(8,128)(2,1)} %maximum_select_fusion.9), channel_id=1, source_target_pairs={{0,2},{2,0},{1,3},{3,1},{4,6},{6,4},{5,7},{7,5},{8,10},{10,8},{9,1... | collective-permute-start | bytes 786440 | tf_op jit(solution)/shard_map/ppermute | solution.py:18
  43.1 14.2 %collective-permute-start.4 = (bf16[2,256,256]{2,1,0:T(8,128)(2,1)}, bf16[2,256,256]{2,1,0:T(8,128)(2,1)}, u32[]{:S(2)}, u32[]{:S(2)}) collective-permute-start(bf16[2,256,256]{2,1,0:T(8,128)(2,1)} %maximum_select_fusion.8), channel_id=1, source_target_pairs={{0,2},{2,0},{1,3},{3,1},{4,6},{6,4},{5,7},{7,5},{8,10},{10,8},{9,1... | collective-permute-start | bytes 786440 | tf_op jit(solution)/shard_map/ppermute | solution.py:18
  58.6 14.8 %collective-permute-start.5 = (bf16[2,512,256]{2,1,0:T(8,128)(2,1)S(1)}, bf16[2,512,256]{2,1,0:T(8,128)(2,1)}, u32[]{:S(2)}, u32[]{:S(2)}) collective-permute-start(bf16[2,512,256]{2,1,0:T(8,128)(2,1)S(1)} %maximum_select_fusion.4), channel_id=1, source_target_pairs={{0,4},{4,0},{1,5},{5,1},{2,6},{6,2},{3,7},{7,3},{8,12},{12,8},{9,1... | collective-permute-start | bytes 1572872 | tf_op jit(solution)/shard_map/ppermute | solution.py:18
  62.5 12.3 %copy-start.19 = (bf16[2,1,16384]{2,0,1:T(2,128)(2,1)S(1)}, bf16[2,1,16384]{2,0,1:T(2,128)(2,1)}, u32[]{:S(2)}) copy-start(bf16[2,1,16384]{2,0,1:T(2,128)(2,1)} %copy.384) | copy-start | bytes 196612
  62.5 12.3 %copy-start.27 = (f32[1,2,8,128]{3,1,2,0:T(2,128)S(1)}, f32[1,2,8,128]{3,1,2,0:T(2,128)}, u32[]{:S(2)}) copy-start(f32[1,2,8,128]{3,1,2,0:T(2,128)} %copy.393) | copy-start | bytes 24580
  62.5 12.3 %copy-start.50 = (f32[2]{0:T(128)S(1)}, f32[2]{0:T(128)}, u32[]{:S(2)}) copy-start(f32[2]{0:T(128)} %copy-done.49) | copy-start | bytes 28
  62.5 12.3 %copy-start.60 = (f32[2,1,128]{2,1,0:T(1,128)S(1)}, f32[2,1,128]{2,1,0:T(1,128)}, u32[]{:S(2)}) copy-start(f32[2,1,128]{2,1,0:T(1,128)} %fusion.177) | copy-start | bytes 3076
  63.3 36.3 %collective-permute-start.11 = (bf16[2,256,256]{2,1,0:T(8,128)(2,1)}, bf16[2,256,256]{2,1,0:T(8,128)(2,1)}, u32[]{:S(2)}, u32[]{:S(2)}) collective-permute-start(bf16[2,256,256]{2,1,0:T(8,128)(2,1)} %fusion.49), channel_id=1, source_target_pairs={{0,2},{2,0},{1,3},{3,1},{4,6},{6,4},{5,7},{7,5},{8,10},{10,8},{9,1... | collective-permute-start | bytes 786440 | tf_op jit(solution)/shard_map/ppermute | solution.py:18
  68.5 23.8 %collective-permute-start.8 = (bf16[2,512,256]{2,1,0:T(8,128)(2,1)}, bf16[2,512,256]{2,1,0:T(8,128)(2,1)}, u32[]{:S(2)}, u32[]{:S(2)}) collective-permute-start(bf16[2,512,256]{2,1,0:T(8,128)(2,1)} %maximum_select_fusion.5), channel_id=1, source_target_pairs={{0,4},{4,0},{1,5},{5,1},{2,6},{6,2},{3,7},{7,3},{8,12},{12,8},{9,1... | collective-permute-start | bytes 1572872 | tf_op jit(solution)/shard_map/ppermute | solution.py:18
  89.4 8.3 %copy-start.6 = (f32[2,256,256]{2,1,0:T(8,128)S(1)}, f32[2,256,256]{2,1,0:T(8,128)}, u32[]{:S(2)}) copy-start(f32[2,256,256]{2,1,0:T(8,128)} %copy-done.5) | copy-start | bytes 1572868
  89.6 15.5 %collective-permute-start.13 = (bf16[2,512,256]{2,1,0:T(8,128)(2,1)S(1)}, bf16[2,512,256]{2,1,0:T(8,128)(2,1)S(1)}, u32[]{:S(2)}, u32[]{:S(2)}) collective-permute-start(bf16[2,512,256]{2,1,0:T(8,128)(2,1)S(1)} %fusion.42), channel_id=1, source_target_pairs={{0,4},{4,0},{1,5},{5,1},{2,6},{6,2},{3,7},{7,3},{8,12},{12,8},{9,1... | collective-permute-start | bytes 1572872 | tf_op jit(solution)/shard_map/ppermute | solution.py:18
  94.0 29.7 %collective-permute-start.9 = (bf16[2,1024,256]{2,1,0:T(8,128)(2,1)S(1)}, bf16[2,1024,256]{2,1,0:T(8,128)(2,1)S(1)}, u32[]{:S(2)}, u32[]{:S(2)}) collective-permute-start(bf16[2,1024,256]{2,1,0:T(8,128)(2,1)S(1)} %maximum_select_fusion.2), channel_id=1, source_target_pairs={{0,8},{8,0},{1,9},{9,1},{2,10},{10,2},{3,11},{11,3},{4,12},{12,4},... | collective-permute-start | bytes 3145736 | tf_op jit(solution)/shard_map/ppermute | solution.py:18
  101.4 60.6 %collective-permute-start.12 = (bf16[2,128,256]{2,1,0:T(8,128)(2,1)}, bf16[2,128,256]{2,1,0:T(8,128)(2,1)}, u32[]{:S(2)}, u32[]{:S(2)}) collective-permute-start(bf16[2,128,256]{2,1,0:T(8,128)(2,1)} %fusion.68), channel_id=1, source_target_pairs={{0,1},{1,0},{2,3},{3,2},{4,5},{5,4},{6,7},{7,6},{8,9},{9,8},{10,11... | collective-permute-start | bytes 393224 | tf_op jit(solution)/shard_map/ppermute | solution.py:18
  105.3 19.0 %copy-start.18 = (bf16[2,1,16384]{2,0,1:T(2,128)(2,1)S(1)}, bf16[2,1,16384]{2,0,1:T(2,128)(2,1)}, u32[]{:S(2)}) copy-start(bf16[2,1,16384]{2,0,1:T(2,128)(2,1)} %copy.388) | copy-start | bytes 196612
  105.3 19.0 %copy-start.48 = (f32[2]{0:T(128)S(1)}, f32[2]{0:T(128)}, u32[]{:S(2)}) copy-start(f32[2]{0:T(128)} %copy-done.47) | copy-start | bytes 28
  105.4 19.0 %copy-start.59 = (f32[2,1,128]{2,1,0:T(1,128)S(1)}, f32[2,1,128]{2,1,0:T(1,128)}, u32[]{:S(2)}) copy-start(f32[2,1,128]{2,1,0:T(1,128)} %fusion.167) | copy-start | bytes 3076
  156.4 5.6 %copy-start.8 = (f32[2,256,256]{2,1,0:T(8,128)S(1)}, f32[2,256,256]{2,1,0:T(8,128)}, u32[]{:S(2)}) copy-start(f32[2,256,256]{2,1,0:T(8,128)} %copy-done.7) | copy-start | bytes 1572868
  158.3 24.5 %collective-permute-start.16 = (bf16[2,1024,256]{2,1,0:T(8,128)(2,1)S(1)}, bf16[2,1024,256]{2,1,0:T(8,128)(2,1)S(1)}, u32[]{:S(2)}, u32[]{:S(2)}) collective-permute-start(bf16[2,1024,256]{2,1,0:T(8,128)(2,1)S(1)} %fusion.36), channel_id=1, source_target_pairs={{0,8},{8,0},{1,9},{9,1},{2,10},{10,2},{3,11},{11,3},{4,12},{12,4},... | collective-permute-start | bytes 3145736 | tf_op jit(solution)/shard_map/ppermute | solution.py:18
  158.5 8.8 %collective-permute-start.14 = (bf16[2,256,256]{2,1,0:T(8,128)(2,1)S(1)}, bf16[2,256,256]{2,1,0:T(8,128)(2,1)S(1)}, u32[]{:S(2)}, u32[]{:S(2)}) collective-permute-start(bf16[2,256,256]{2,1,0:T(8,128)(2,1)S(1)} %fusion.50), channel_id=1, source_target_pairs={{0,2},{2,0},{1,3},{3,1},{4,6},{6,4},{5,7},{7,5},{8,10},{10,8},{9,1... | collective-permute-start | bytes 786440 | tf_op jit(solution)/shard_map/ppermute | solution.py:18
  161.8 21.0 %copy-start = (f32[2,1,1024,256]{3,2,0,1:T(8,128)S(1)}, f32[2,1,1024,256]{3,2,0,1:T(8,128)}, u32[]{:S(2)}) copy-start(f32[2,1,1024,256]{3,2,0,1:T(8,128)} %copy.158) | copy-start | bytes 6291460
  167.4 16.4 %copy-start.12 = (bf16[2,1024,256]{2,1,0:T(8,128)(2,1)S(1)}, bf16[2,1024,256]{2,1,0:T(8,128)(2,1)}, u32[]{:S(2)}) copy-start(bf16[2,1024,256]{2,1,0:T(8,128)(2,1)} %copy-done.11) | copy-start | bytes 3145732
  167.4 16.4 %copy-start.16 = (bf16[2,128,1024]{2,1,0:T(8,128)(2,1)S(1)}, bf16[2,128,1024]{2,1,0:T(8,128)(2,1)}, u32[]{:S(2)}) copy-start(bf16[2,128,1024]{2,1,0:T(8,128)(2,1)} %copy-done.15) | copy-start | bytes 1572868
  167.4 16.8 %collective-permute-start.15 = (bf16[2,128,256]{2,1,0:T(8,128)(2,1)S(1)}, bf16[2,128,256]{2,1,0:T(8,128)(2,1)S(1)}, u32[]{:S(2)}, u32[]{:S(2)}) collective-permute-start(bf16[2,128,256]{2,1,0:T(8,128)(2,1)S(1)} %fusion.69), channel_id=1, source_target_pairs={{0,1},{1,0},{2,3},{3,2},{4,5},{5,4},{6,7},{7,6},{8,9},{9,8},{10,11... | collective-permute-start | bytes 393224 | tf_op jit(solution)/shard_map/ppermute | solution.py:18
  183.3 9.3 %collective-permute-start.17 = (bf16[2,512,256]{2,1,0:T(8,128)(2,1)S(1)}, bf16[2,512,256]{2,1,0:T(8,128)(2,1)S(1)}, u32[]{:S(2)}, u32[]{:S(2)}) collective-permute-start(bf16[2,512,256]{2,1,0:T(8,128)(2,1)S(1)} %fusion.43), channel_id=1, source_target_pairs={{0,4},{4,0},{1,5},{5,1},{2,6},{6,2},{3,7},{7,3},{8,12},{12,8},{9,1... | collective-permute-start | bytes 1572872 | tf_op jit(solution)/shard_map/ppermute | solution.py:18
  185.6 11.7 %copy-start.20 = (f32[2,2,16384]{2,1,0:T(2,128)S(1)}, f32[2,2,16384]{2,1,0:T(2,128)}, u32[]{:S(2)}) copy-start(f32[2,2,16384]{2,1,0:T(2,128)} %reshape_reshape_transpose.2) | copy-start | bytes 786436
  185.6 11.7 %copy-start.26 = (f32[1,2,128,128]{3,1,2,0:T(2,128)S(1)}, f32[1,2,128,128]{3,1,2,0:T(2,128)}, u32[]{:S(2)}) copy-start(f32[1,2,128,128]{3,1,2,0:T(2,128)} %copy.373) | copy-start | bytes 393220
  185.6 11.7 %copy-start.52 = (f32[2,2]{1,0:T(2,128)S(1)}, f32[2,2]{1,0:T(2,128)}, u32[]{:S(2)}) copy-start(f32[2,2]{1,0:T(2,128)} %copy-done.51) | copy-start | bytes 52
  185.6 11.7 %copy-start.53 = (f32[2,2]{1,0:T(2,128)S(1)}, f32[2,2]{1,0:T(2,128)}, u32[]{:S(2)}) copy-start(f32[2,2]{1,0:T(2,128)} %get-tuple-element.207) | copy-start | bytes 52
  185.6 11.7 %copy-start.54 = (f32[2,2]{1,0:T(2,128)S(1)}, f32[2,2]{1,0:T(2,128)}, u32[]{:S(2)}) copy-start(f32[2,2]{1,0:T(2,128)} %get-tuple-element.208) | copy-start | bytes 52
  185.6 11.7 %copy-start.55 = (f32[2,2]{1,0:T(2,128)S(1)}, f32[2,2]{1,0:T(2,128)}, u32[]{:S(2)}) copy-start(f32[2,2]{1,0:T(2,128)} %get-tuple-element.203) | copy-start | bytes 52
  185.6 11.7 %copy-start.56 = (f32[2,2]{1,0:T(2,128)S(1)}, f32[2,2]{1,0:T(2,128)}, u32[]{:S(2)}) copy-start(f32[2,2]{1,0:T(2,128)} %get-tuple-element.204) | copy-start | bytes 52
  185.6 11.7 %copy-start.58 = (s32[2,2]{1,0:T(2,128)S(1)}, s32[2,2]{1,0:T(2,128)}, u32[]{:S(2)}) copy-start(s32[2,2]{1,0:T(2,128)} %copy-done.57) | copy-start | bytes 52
  193.5 55.0 %collective-permute-start.18 = (bf16[2,256,256]{2,1,0:T(8,128)(2,1)}, bf16[2,256,256]{2,1,0:T(8,128)(2,1)S(1)}, u32[]{:S(2)}, u32[]{:S(2)}) collective-permute-start(bf16[2,256,256]{2,1,0:T(8,128)(2,1)} %fusion.51), channel_id=1, source_target_pairs={{0,2},{2,0},{1,3},{3,1},{4,6},{6,4},{5,7},{7,5},{8,10},{10,8},{9,1... | collective-permute-start | bytes 786440 | tf_op jit(solution)/shard_map/ppermute | solution.py:18
  198.6 51.5 %copy-start.37 = (f32[256]{0:T(256)S(1)}, f32[256]{0:T(256)}, u32[]{:S(2)}) copy-start(f32[256]{0:T(256)} %param.13) | copy-start | bytes 3076
  199.3 55.1 %copy-start.17 = (f32[2,2,32768]{2,1,0:T(2,128)S(1)}, f32[2,2,32768]{2,1,0:T(2,128)}, u32[]{:S(2)}) copy-start(f32[2,2,32768]{2,1,0:T(2,128)} %reshape.1667) | copy-start | bytes 1572868
  199.3 55.1 %copy-start.21 = (f32[1,2,128,256]{3,1,2,0:T(2,128)S(1)}, f32[1,2,128,256]{3,1,2,0:T(2,128)}, u32[]{:S(2)}) copy-start(f32[1,2,128,256]{3,1,2,0:T(2,128)} %copy.191) | copy-start | bytes 786436
  199.3 55.1 %copy-start.22 = (f32[1,2,128,256]{3,1,2,0:T(2,128)S(1)}, f32[1,2,128,256]{3,1,2,0:T(2,128)}, u32[]{:S(2)}) copy-start(f32[1,2,128,256]{3,1,2,0:T(2,128)} %copy.192) | copy-start | bytes 786436
  248.7 5.5 %collective-permute-start.19 = (bf16[2,128,256]{2,1,0:T(8,128)(2,1)S(1)}, bf16[2,128,256]{2,1,0:T(8,128)(2,1)S(1)}, u32[]{:S(2)}, u32[]{:S(2)}) collective-permute-start(bf16[2,128,256]{2,1,0:T(8,128)(2,1)S(1)} %fusion.70), channel_id=1, source_target_pairs={{0,1},{1,0},{2,3},{3,2},{4,5},{5,4},{6,7},{7,6},{8,9},{9,8},{10,11... | collective-permute-start | bytes 393224 | tf_op jit(solution)/shard_map/ppermute | solution.py:18
  (19 other events, 52.2 us)
